TPU v7x, 32 devices: a whole 2x2x4 slice. The times are simulated.
32 devices in a mesh: group: 4 (over y, x), member: 8 (over z, core).
Axes of the slice: x: 2, y: 2, z: 4, core: 2. Of those that a mesh axis runs over, the one named last changes fastest.
Arguments:
- picture_embedding_matrix: bfloat16 [8192, 1152], P(('group', 'member')), may hold values from -1 to 1
- caption_embedding_matrix: bfloat16 [8192, 1152], P(('group', 'member')), may hold values from -1 to 1
- learned_sharpness: float32 [1], replicated, may hold values from 5 to 20
- learned_offset_entry: float32 [1], replicated, may hold values from -4 to -2
Outputs:
- grad_images: float32 [8192, 1152], P(('group', 'member'))
- grad_texts: float32 [8192, 1152], P(('group', 'member'))
All inputs are finite; a program needn't handle non-finite values.
Results may differ from a plain program's by a relative error of at most 0.002.
Values may be sent and summed in bfloat16 or wider, within the bound.
A program may use at most 192 MiB of HBM per device.

v0:
```python
import jax
import jax.numpy as jnp
from jax import lax
from jax.sharding import PartitionSpec as P


def passed_along(shard, axis, by):
    devices = lax.axis_size(axis)
    return lax.ppermute(shard, axis, [(i, (i + by) % devices) for i in range(devices)])


def weighting_factors(similarity_scores, match_polarity, sharpness_multiplier):
    return (
        -sharpness_multiplier * match_polarity * jax.nn.sigmoid(-match_polarity * similarity_scores)
    ).astype(jnp.bfloat16)


def shards(
    picture_embedding_matrix, caption_embedding_matrix, learned_sharpness, learned_offset_entry
):
    sharpness_multiplier = learned_sharpness[0]
    offset_amount = learned_offset_entry[0]
    count_of_rows = picture_embedding_matrix.shape[0]
    member_idx = lax.axis_index("member")
    members = lax.axis_size("member")
    columns = lax.broadcasted_iota(jnp.int32, (count_of_rows, count_of_rows * members), 1)
    targets = (
        lax.broadcasted_iota(jnp.int32, (count_of_rows, count_of_rows * members), 0)
        + member_idx * count_of_rows
    )
    match_polarity = jnp.where(columns == targets, 1.0, -1.0).astype(jnp.float32)
    txt_prev = passed_along(caption_embedding_matrix, "group", 1)
    earlier_scores = (
        sharpness_multiplier
        * jnp.dot(picture_embedding_matrix, txt_prev.T, preferred_element_type=jnp.float32)
        + offset_amount
    )
    earlier_multipliers = weighting_factors(earlier_scores, -1.0, sharpness_multiplier)
    grad_prev = jnp.dot(earlier_multipliers, txt_prev, preferred_element_type=jnp.float32)
    group_text_rows, group_img = (
        lax.all_gather(caption_embedding_matrix, "member", axis=0, tiled=True),
        lax.all_gather(picture_embedding_matrix, "member", axis=0, tiled=True),
    )
    similarity_scores = (
        sharpness_multiplier
        * jnp.dot(picture_embedding_matrix, group_text_rows.T, preferred_element_type=jnp.float32)
        + offset_amount
    )
    score_multipliers = weighting_factors(similarity_scores, match_polarity, sharpness_multiplier)
    grad_images = (
        jnp.dot(score_multipliers, group_text_rows, preferred_element_type=jnp.float32) + grad_prev
    )
    text_logits = (
        sharpness_multiplier
        * jnp.dot(caption_embedding_matrix, group_img.T, preferred_element_type=jnp.float32)
        + offset_amount
    )
    text_coeffs = weighting_factors(text_logits, match_polarity, sharpness_multiplier)
    img_next = passed_along(picture_embedding_matrix, "group", -1)
    next_logits = (
        sharpness_multiplier
        * jnp.dot(caption_embedding_matrix, img_next.T, preferred_element_type=jnp.float32)
        + offset_amount
    )
    next_coeffs = weighting_factors(next_logits, -1.0, sharpness_multiplier)
    grad_texts = jnp.dot(text_coeffs, group_img, preferred_element_type=jnp.float32)
    grad_texts = grad_texts + jnp.dot(next_coeffs, img_next, preferred_element_type=jnp.float32)
    return (grad_images, grad_texts)


def solution(mesh):
    in_specs = (P(("group", "member"), None), P(("group", "member"), None), P(), P())
    out_specs = (P(("group", "member"), None), P(("group", "member"), None))
    return jax.shard_map(shards, mesh=mesh, in_specs=in_specs, out_specs=out_specs, check_vma=False)
```

profile of v0, /device:TPU:0, one launch (start us, length us, event | category | flops | bytes accessed | tf_op | source)
XLA Modules:
  0.0 134.1 jit_solution(1650488425485670412)
XLA Ops:
  7.2 0.0 all-gather.5.cloned.1.call-start
  7.2 0.7 all-gather.5.cloned.1.call-update
  7.9 0.0 all-gather.3.cloned.1.call-start
  7.9 0.7 all-gather.3.cloned.1.call-update
  8.6 4.0 %collective-permute-start.1 = (bf16[256,1152]{1,0:T(8,128)(2,1)}, bf16[256,1152]{1,0:T(8,128)(2,1)S(1)}, u32[]{:S(2)}, u32[]{:S(2)}) collective-permute-start(bf16[256,1152]{1,0:T(8,128)(2,1)} %param.4), channel_id=1, source_target_pairs={{0,24},{8,0},{16,8},{24,16},{1,25},{9,1},{17,9},{25,17},{2,26},{10... | collective-permute-start | bytes 1769480 | tf_op jit(solution)/shard_map/ppermute | solution.py:9
  12.6 0.0 collective-permute-start
  13.9 49.6 %all-gather.5.cloned.1.call-done = bf16[2048,1152]{1,0:T(8,128)(2,1)} async-done(((bf16[256,1152]{1,0:T(8,128)(2,1)}), bf16[2048,1152]{1,0:T(8,128)(2,1)}) %all-gather.5.cloned.1.call-update) | async-done | bytes 4718608 | tf_op jit(solution)/shard_map/all_gather | solution.py:42
  63.6 0.0 copy-start.1
  63.6 8.1 %fusion.17 = f32[256,1152]{1,0:T(8,128)} fusion(bf16[2048,1152]{1,0:T(8,128)(2,1)} %all-gather.5.cloned.1.call-done, bf16[256,1152]{1,0:T(8,128)(2,1)} %param.5, f32[]{:T(128)} %bitcast.21, f32[]{:T(128)} %bitcast.17, s32[256]{0:T(256)S(1)} %iota_add_fusion, f32[]{:T(128)S(6)} %neg.22), kind=kOutput, calls=%fused_computation.24 | convolution fusion | flops 2422210560 | bytes 6489100 | tf_op jit(solution)/shard_map/dot_general | solution.py:66
  71.7 43.6 %all-gather.3.cloned.1.call-done = bf16[2048,1152]{1,0:T(8,128)(2,1)} async-done(((bf16[256,1152]{1,0:T(8,128)(2,1)}), bf16[2048,1152]{1,0:T(8,128)(2,1)}) %all-gather.3.cloned.1.call-update) | async-done | bytes 4718608 | tf_op jit(solution)/shard_map/all_gather | solution.py:41
  115.2 0.0 copy-done.1
  115.2 0.0 copy-start
  115.2 6.9 %fusion.16 = f32[256,1152]{1,0:T(8,128)S(1)} fusion(bf16[2048,1152]{1,0:T(8,128)(2,1)} %all-gather.3.cloned.1.call-done, bf16[256,1152]{1,0:T(8,128)(2,1)S(1)} %copy-done.1, f32[]{:T(128)} %bitcast.19, f32[]{:T(128)} %bitcast.15, s32[256]{0:T(256)S(1)} %iota_add_fusion, f32[]{:T(128)S(6)} %neg.22), kind=kOutput, calls=%fused_computation.23 | convolution fusion | flops 2422210560 | bytes 6489100 | tf_op jit(solution)/shard_map/dot_general | solution.py:51
  122.1 0.0 collective-permute-done.1
  122.1 0.0 copy-done
  122.1 3.2 %convolution_add_fusion = f32[256,1152]{1,0:T(8,128)} fusion(f32[256,1152]{1,0:T(8,128)} %fusion.17, bf16[256,1152]{1,0:T(8,128)(2,1)S(1)} %collective-permute-done.1, bf16[256,1152]{1,0:T(8,128)(2,1)S(1)} %copy-done, f32[]{:T(128)} %bitcast.22, f32[]{:T(128)} %bitcast.18, f32[]{:T(128)S(6)} %mul.64), kind=kOutput, calls=%fused_computation | convolution fusion | flops 302743552 | bytes 3538956 | tf_op jit(solution)/shard_map/dot_general | solution.py:67
  125.4 0.0 collective-permute-done
  125.4 1.9 %convolution_add_fusion.1 = f32[256,1152]{1,0:T(8,128)} fusion(f32[256,1152]{1,0:T(8,128)S(1)} %fusion.16, bf16[256,1152]{1,0:T(8,128)(2,1)S(1)} %collective-permute-done, bf16[256,1152]{1,0:T(8,128)(2,1)S(1)} %copy-done.1, f32[]{:T(128)} %bitcast.20, f32[]{:T(128)} %bitcast.16, f32[]{:T(128)S(6)} %mul.64), kind=kOutput, calls=%fused_computation.1 | convolution fusion | flops 302743552 | bytes 3538956 | tf_op jit(solution)/shard_map/dot_general | solution.py:39
  (1 shorter events, 0.0 us)
Async XLA Ops:
  7.2 56.4 %all-gather.5.cloned.1.call-start = ((), (), s32[]{:S(2)}) async-start(), calls=%async_computation.1 | async-start | bytes 5308416 | tf_op jit(solution)/shard_map/all_gather | solution.py:42
  7.9 107.3 %all-gather.3.cloned.1.call-start = ((), (), s32[]{:S(2)}) async-start(), calls=%async_computation | async-start | bytes 5308416 | tf_op jit(solution)/shard_map/all_gather | solution.py:41
  8.6 113.5 %collective-permute-start.1 = (bf16[256,1152]{1,0:T(8,128)(2,1)}, bf16[256,1152]{1,0:T(8,128)(2,1)S(1)}, u32[]{:S(2)}, u32[]{:S(2)}) collective-permute-start(bf16[256,1152]{1,0:T(8,128)(2,1)} %param.4), channel_id=1, source_target_pairs={{0,24},{8,0},{16,8},{24,16},{1,25},{9,1},{17,9},{25,17},{2,26},{10... | collective-permute-start | bytes 1769480 | tf_op jit(solution)/shard_map/ppermute | solution.py:9
  12.6 112.7 %collective-permute-start = (bf16[256,1152]{1,0:T(8,128)(2,1)}, bf16[256,1152]{1,0:T(8,128)(2,1)S(1)}, u32[]{:S(2)}, u32[]{:S(2)}) collective-permute-start(bf16[256,1152]{1,0:T(8,128)(2,1)} %param.5), channel_id=1, source_target_pairs={{0,8},{8,16},{16,24},{24,0},{1,9},{9,17},{17,25},{25,1},{2,10},{10... | collective-permute-start | bytes 1769480 | tf_op jit(solution)/shard_map/ppermute | solution.py:9
  63.6 51.6 %copy-start.1 = (bf16[256,1152]{1,0:T(8,128)(2,1)S(1)}, bf16[256,1152]{1,0:T(8,128)(2,1)}, u32[]{:S(2)}) copy-start(bf16[256,1152]{1,0:T(8,128)(2,1)} %param.4) | copy-start | bytes 1769476
  115.2 6.9 %copy-start = (bf16[256,1152]{1,0:T(8,128)(2,1)S(1)}, bf16[256,1152]{1,0:T(8,128)(2,1)}, u32[]{:S(2)}) copy-start(bf16[256,1152]{1,0:T(8,128)(2,1)} %param.5) | copy-start | bytes 1769476
Sparse Core Ops, SparseCore 0:
  9.6 53.9 all-gather.4
  65.2 49.9 all-gather.2
where the time goes:
time: 134 us
  waiting for transfers between devices  94.6 us (71%)
  matrix products  20.1 us (15%)
  between operations  15.4 us (11%)
  starting transfers between devices  4.05 us (3%)
    all_gather x1, waiting for transfers between devices, shards(): lax.all_gather(picture_embedding_matrix, 'member', axis=0, tiled=True)  49.6 us
    all_gather x1, waiting for transfers between devices, shards(): lax.all_gather(caption_embedding_matrix, 'member', axis=0, tiled=True)  43.6 us
    dot_general x1, matrix products, shards(): jnp.dot(text_coeffs, group_img, preferred_element_type=jnp.float32)  8.07 us
    dot_general x1, matrix products, shards(): jnp.dot(score_multipliers, group_text_rows, preferred_element_type=jnp.fl...  6.88 us
    ppermute x2, starting transfers between devices, passed_along(): lax.ppermute(shard, axis, [(i, (i + by) % devices) for i in range(devices)])  3.98 us
    dot_general x1, matrix products, shards(): jnp.dot(next_coeffs, img_next, preferred_element_type=jnp.float32)  3.22 us
  transfers between devices with their start and end apart: 4, of which 2 were waited for; matrix products, arithmetic and copies ran while one was open for 14% of the time, Pallas kernels for 0%

commit v1 on v0

--- a/solution.py
+++ b/solution.py
@@ -37,9 +37,17 @@
     )
     earlier_multipliers = weighting_factors(earlier_scores, -1.0, sharpness_multiplier)
     grad_prev = jnp.dot(earlier_multipliers, txt_prev, preferred_element_type=jnp.float32)
+
+    def touch_rows_up(mine_x):
+        left_arr = lax.axis_size("member")
+        latest = jnp.stack(left_arr * [mine_x])
+        o_now = lax.all_to_all(latest, "member", concat_axis=0, split_axis=0)
+        found_now = jnp.concatenate(o_now, axis=0)
+        return found_now
+
     group_text_rows, group_img = (
         lax.all_gather(caption_embedding_matrix, "member", axis=0, tiled=True),
-        lax.all_gather(picture_embedding_matrix, "member", axis=0, tiled=True),
+        touch_rows_up(picture_embedding_matrix),
     )
     similarity_scores = (
         sharpness_multiplier

time: 134 us -> 188 us (1.40)
  waiting for transfers between devices: 94.6 us -> 139 us
  starting transfers between devices: 4.05 us -> 9.02 us
  local copies, waits for them, and re-layouts: 0.01 us -> 3.9 us
    all_to_all x0 -> x1, waiting for transfers between devices: none -> 139 us  [touch_rows_up(): o_now = lax.all_to_all(latest, 'member', concat_axis=0, split_axis=0)]
    all_gather x1 -> x0, waiting for transfers between devices: 49.6 us -> none  [shards(): lax.all_gather(picture_embedding_matrix, 'member', axis=0, tiled=True)]
    all_gather x1, waiting for transfers between devices: 43.6 us -> 0.01 us  [shards(): lax.all_gather(caption_embedding_matrix, 'member', axis=0, tiled=True)]
    all_to_all x0 -> x1, starting transfers between devices: none -> 6.49 us  [touch_rows_up(): o_now = lax.all_to_all(latest, 'member', concat_axis=0, split_axis=0)]
    another operation x0 -> x1, local copies, waits for them, and re-layouts: none -> 3.89 us  [touch_rows_up(): latest = jnp.stack(left_arr * [mine_x])]
  transfers between devices with their start and end apart: 4 -> 4, of which waited for: 2 -> 1; matrix products, arithmetic and copies ran while one was open for 14% -> 10% of each run, Pallas kernels for 0% -> 0%
where the time goes in v1:
time: 188 us
  waiting for transfers between devices  139 us (74%)
  matrix products  19.9 us (11%)
  between operations  15.4 us (8%)
  starting transfers between devices  9.02 us (5%)
  local copies, waits for them, and re-layouts  3.9 us (2%)
    all_to_all x1, waiting for transfers between devices, touch_rows_up(): o_now = lax.all_to_all(latest, 'member', concat_axis=0, split_axis=0)  139 us
    dot_general x1, matrix products, shards(): jnp.dot(text_coeffs, group_img, preferred_element_type=jnp.float32)  7.86 us
    dot_general x1, matrix products, shards(): jnp.dot(score_multipliers, group_text_rows, preferred_element_type=jnp.fl...  6.84 us
    all_to_all x1, starting transfers between devices, touch_rows_up(): o_now = lax.all_to_all(latest, 'member', concat_axis=0, split_axis=0)  6.49 us
    another operation x1, local copies, waits for them, and re-layouts, touch_rows_up(): latest = jnp.stack(left_arr * [mine_x])  3.89 us
  transfers between devices with their start and end apart: 4, of which 1 were waited for; matrix products, arithmetic and copies ran while one was open for 10% of the time, Pallas kernels for 0%

profile of v1, /device:TPU:0, one launch (start us, length us, event | category | flops | bytes accessed | tf_op | source)
XLA Modules:
  0.0 187.5 jit_solution(11321508338770350572)
XLA Ops:
  7.2 3.9 %stack.2 = bf16[8,256,1152]{2,1,0:T(8,128)(2,1)} broadcast(bf16[256,1152]{1,0:T(8,128)(2,1)} %param.4), dimensions={1,2} | broadcast | bytes 5308416 | tf_op jit(solution)/shard_map/stack | solution.py:43
  11.1 0.0 copy-start.1
  11.1 0.0 copy-start
  11.1 6.5 %all-to-all-start = ((bf16[8,256,1152]{2,1,0:T(8,128)(2,1)}), bf16[8,256,1152]{2,1,0:T(8,128)(2,1)}, u32[]{:S(2)}, u32[]{:S(2)}) async-start(bf16[8,256,1152]{2,1,0:T(8,128)(2,1)} %stack.2), calls=%async_computation | async-start | bytes 9437184 | tf_op jit(solution)/shard_map/all_to_all | solution.py:44
  17.5 0.0 all-gather.2.cloned.1.call-start
  17.6 0.7 all-gather.2.cloned.1.call-update
  18.3 0.0 copy-done.1
  18.3 2.5 %collective-permute-start.1 = (bf16[256,1152]{1,0:T(8,128)(2,1)S(1)}, bf16[256,1152]{1,0:T(8,128)(2,1)S(1)}, u32[]{:S(2)}, u32[]{:S(2)}) collective-permute-start(bf16[256,1152]{1,0:T(8,128)(2,1)S(1)} %copy-done.1), channel_id=1, source_target_pairs={{0,24},{8,0},{16,8},{24,16},{1,25},{9,1},{17,9},{25,17},{2,26},{10... | collective-permute-start | bytes 1769480 | tf_op jit(solution)/shard_map/ppermute | solution.py:9
  20.8 0.0 copy-done
  20.8 0.0 collective-permute-start
  22.1 138.7 %all-to-all-done = bf16[8,256,1152]{2,1,0:T(8,128)(2,1)} async-done(((bf16[8,256,1152]{2,1,0:T(8,128)(2,1)}), bf16[8,256,1152]{2,1,0:T(8,128)(2,1)}, u32[]{:S(2)}, u32[]{:S(2)}) %all-to-all-start) | async-done | bytes 4718624 | tf_op jit(solution)/shard_map/all_to_all | solution.py:44
  160.8 7.9 %fusion.17 = f32[256,1152]{1,0:T(8,128)} fusion(bf16[2048,1152]{1,0:T(8,128)(2,1)} %bitcast.2, bf16[256,1152]{1,0:T(8,128)(2,1)S(1)} %copy-done, f32[]{:T(128)} %bitcast.22, f32[]{:T(128)} %bitcast.18, s32[256]{0:T(256)S(1)} %iota_add_fusion, f32[]{:T(128)S(6)} %neg.22), kind=kOutput, calls=%fused_computation.24 | convolution fusion | flops 2422210560 | bytes 6489100 | tf_op jit(solution)/shard_map/dot_general | solution.py:74
  168.6 0.0 all-gather.2.cloned.1.call-done
  168.6 6.8 %fusion.16 = f32[256,1152]{1,0:T(8,128)S(1)} fusion(bf16[2048,1152]{1,0:T(8,128)(2,1)} %all-gather.2.cloned.1.call-done, bf16[256,1152]{1,0:T(8,128)(2,1)S(1)} %copy-done.1, f32[]{:T(128)} %bitcast.20, f32[]{:T(128)} %bitcast.16, s32[256]{0:T(256)S(1)} %iota_add_fusion, f32[]{:T(128)S(6)} %neg.22), kind=kOutput, calls=%fused_computation.23 | convolution fusion | flops 2422210560 | bytes 6489100 | tf_op jit(solution)/shard_map/dot_general | solution.py:59
  175.5 0.0 collective-permute-done.1
  175.5 3.2 %convolution_add_fusion = f32[256,1152]{1,0:T(8,128)} fusion(f32[256,1152]{1,0:T(8,128)} %fusion.17, bf16[256,1152]{1,0:T(8,128)(2,1)S(1)} %collective-permute-done.1, bf16[256,1152]{1,0:T(8,128)(2,1)S(1)} %copy-done, f32[]{:T(128)} %bitcast.23, f32[]{:T(128)} %bitcast.19, f32[]{:T(128)S(6)} %mul.64), kind=kOutput, calls=%fused_computation | convolution fusion | flops 302743552 | bytes 3538956 | tf_op jit(solution)/shard_map/dot_general | solution.py:75
  178.7 0.0 collective-permute-done
  178.7 1.9 %convolution_add_fusion.1 = f32[256,1152]{1,0:T(8,128)} fusion(f32[256,1152]{1,0:T(8,128)S(1)} %fusion.16, bf16[256,1152]{1,0:T(8,128)(2,1)S(1)} %collective-permute-done, bf16[256,1152]{1,0:T(8,128)(2,1)S(1)} %copy-done.1, f32[]{:T(128)} %bitcast.21, f32[]{:T(128)} %bitcast.17, f32[]{:T(128)S(6)} %mul.64), kind=kOutput, calls=%fused_computation.1 | convolution fusion | flops 302743552 | bytes 3538956 | tf_op jit(solution)/shard_map/dot_general | solution.py:39
  (1 shorter events, 0.0 us)
Async XLA Ops:
  11.1 7.2 %copy-start.1 = (bf16[256,1152]{1,0:T(8,128)(2,1)S(1)}, bf16[256,1152]{1,0:T(8,128)(2,1)}, u32[]{:S(2)}) copy-start(bf16[256,1152]{1,0:T(8,128)(2,1)} %param.4) | copy-start | bytes 1769476
  11.1 9.7 %copy-start = (bf16[256,1152]{1,0:T(8,128)(2,1)S(1)}, bf16[256,1152]{1,0:T(8,128)(2,1)}, u32[]{:S(2)}) copy-start(bf16[256,1152]{1,0:T(8,128)(2,1)} %param.5) | copy-start | bytes 1769476
  11.1 149.7 %all-to-all-start = ((bf16[8,256,1152]{2,1,0:T(8,128)(2,1)}), bf16[8,256,1152]{2,1,0:T(8,128)(2,1)}, u32[]{:S(2)}, u32[]{:S(2)}) async-start(bf16[8,256,1152]{2,1,0:T(8,128)(2,1)} %stack.2), calls=%async_computation | async-start | bytes 9437184 | tf_op jit(solution)/shard_map/all_to_all | solution.py:44
  17.5 151.1 %all-gather.2.cloned.1.call-start = ((), (), s32[]{:S(2)}) async-start(), calls=%async_computation.1 | async-start | bytes 5308416 | tf_op jit(solution)/shard_map/all_gather | solution.py:49
  18.3 157.2 %collective-permute-start.1 = (bf16[256,1152]{1,0:T(8,128)(2,1)S(1)}, bf16[256,1152]{1,0:T(8,128)(2,1)S(1)}, u32[]{:S(2)}, u32[]{:S(2)}) collective-permute-start(bf16[256,1152]{1,0:T(8,128)(2,1)S(1)} %copy-done.1), channel_id=1, source_target_pairs={{0,24},{8,0},{16,8},{24,16},{1,25},{9,1},{17,9},{25,17},{2,26},{10... | collective-permute-start | bytes 1769480 | tf_op jit(solution)/shard_map/ppermute | solution.py:9
  20.8 157.9 %collective-permute-start = (bf16[256,1152]{1,0:T(8,128)(2,1)S(1)}, bf16[256,1152]{1,0:T(8,128)(2,1)S(1)}, u32[]{:S(2)}, u32[]{:S(2)}) collective-permute-start(bf16[256,1152]{1,0:T(8,128)(2,1)S(1)} %copy-done), channel_id=1, source_target_pairs={{0,8},{8,16},{16,24},{24,0},{1,9},{9,17},{17,25},{25,1},{2,10},{10... | collective-permute-start | bytes 1769480 | tf_op jit(solution)/shard_map/ppermute | solution.py:9
Sparse Core Ops, SparseCore 0:
  20.0 90.0 all-gather.1
